TPU v7x, 128 devices: a whole 4x4x4 slice. The times are simulated.
128 devices in a mesh: row: 8 (over x, z_lo), col: 16 (over z_hi, y, core).
Axes of the slice: x: 4, y: 4, z: 4 (z_hi: 2, z_lo: 2; z = z_hi * 2 + z_lo), core: 2. Of those that a mesh axis runs over, the one named last changes fastest.
Arguments:
- amplitudes: bfloat16 [32, 768, 768], P('row', 'col'), may hold values from -6 to 6
- factors: bfloat16 [64, 768, 768], P('col', 'row'), may hold values from -0.109375 to 0.109375
- counts: int32 [8], replicated, may hold values from 1 to 4, 16 in all
- pair_index: int32 [32, 2], replicated, may hold values from 0 to 23
- occ_energy: float32 [24], replicated, may hold values from -2 to -0.5
- vir_energy: float32 [768], replicated, may hold values from 0.5 to 3
Outputs:
- new_amplitudes: bfloat16 [32, 768, 768], P('row', 'col')
Inputs may be any that keep to these rules, and one draw needn't show every extreme that they name: The counts sum to 2 times the number of owner rows. `pair_index`: entries of slots that are not live are not used.
All inputs are finite; a program needn't handle non-finite values.
Results may differ from a plain program's by a relative error of at most 0.0046.
Values may be sent and summed in bfloat16 or wider, within the bound.
No kernel may reach another device: no remote copies, remote signals or barrier semaphores. Data moves between devices by JAX's collectives and lax.ppermute only.
A program may use at most 64 MiB of HBM per device.

v0:
```python
import jax
import jax.numpy as jnp
from jax import lax
from jax.sharding import PartitionSpec as P

level_shift = 1.0


def per_device(amplitudes, factors, counts, pair_index, occ_energy, vir_energy):
    slot_count = amplitudes.shape[0]
    col_rows = amplitudes.shape[1]
    row_id = lax.axis_index("row")
    col_id = lax.axis_index("col")
    full_factors = lax.all_gather(factors, "row", axis=1, tiled=True)
    local_slots = jnp.arange(slot_count, dtype=jnp.int32)
    own_live = local_slots < counts[row_id]
    held_pairs = lax.dynamic_slice_in_dim(pair_index, row_id * slot_count, slot_count, 0)
    halfway = jnp.einsum(
        "scb,qdb->sqcd",
        lax.all_gather(amplitudes, "col", axis=1, tiled=True),
        full_factors,
        preferred_element_type=jnp.float32,
    ).astype(jnp.bfloat16)
    ladder = lax.psum_scatter(
        jnp.einsum("qac,sqcd->asd", full_factors, halfway, preferred_element_type=jnp.float32),
        "col",
        scatter_dimension=0,
        tiled=True,
    )
    ladder = jnp.transpose(ladder, (1, 0, 2))
    row_energy = lax.dynamic_slice_in_dim(vir_energy, col_id * col_rows, col_rows, 0)
    occupied = jnp.arange(occ_energy.shape[0], dtype=jnp.int32)
    picks = (held_pairs[:, :, None] == occupied[None, None, :]).astype(jnp.float32)
    pair_energy = jnp.sum(picks * occ_energy[None, None, :], axis=(1, 2))
    denominator = row_energy[None, :, None] + vir_energy[None, None, :] - pair_energy[:, None, None]
    amps_float = amplitudes.astype(jnp.float32)
    updated = amps_float - (ladder + denominator * amps_float) / (denominator + level_shift)
    updated = jnp.where(own_live[:, None, None], updated, 0.0).astype(jnp.bfloat16)
    return updated


def solution(mesh):
    in_specs = (P("row", "col", None), P("col", "row", None), P(), P(), P(), P())
    out_specs = P("row", "col", None)
    return jax.shard_map(
        per_device, mesh=mesh, in_specs=in_specs, out_specs=out_specs, check_vma=False
    )
```

profile of v0, /device:TPU:0, one launch (start us, length us, event | category | flops | bytes accessed | tf_op | source)
XLA Modules:
  0.0 402.4 jit_solution(1089132526216509882)
XLA Ops:
  6.5 0.0 copy-start
  6.5 0.0 all-gather.3.cloned.1.call-start
  6.5 0.7 all-gather.3.cloned.1.call-update
  7.3 0.0 all-gather.5.cloned.1.call-start
  7.3 0.7 all-gather.5.cloned.1.call-update
  8.0 0.0 all-reduce.3.cloned.1.call-start
  8.1 103.0 %all-gather.3.cloned.1.call-done = bf16[4,768,768]{2,1,0:T(8,128)(2,1)} async-done(((bf16[4,96,768]{2,1,0:T(8,128)(2,1)}), bf16[4,768,768]{2,1,0:T(8,128)(2,1)}) %all-gather.3.cloned.1.call-update) | async-done | bytes 4718608 | tf_op jit(solution)/shard_map/all_gather | solution.py:14
  111.1 61.7 %all-gather.5.cloned.1.call-done = bf16[4,768,768]{2,1,0:T(8,128)(2,1)} async-done(((bf16[4,48,768]{2,1,0:T(8,128)(2,1)}), bf16[4,768,768]{2,1,0:T(8,128)(2,1)}) %all-gather.5.cloned.1.call-update) | async-done | bytes 4718608 | tf_op jit(solution)/shard_map/all_gather | solution.py:20
  172.7 42.8 %fusion.7 = f32[768,4,768]{0,2,1:T(8,128)} fusion(bf16[4,768,768]{2,1,0:T(8,128)(2,1)} %all-gather.3.cloned.1.call-done, bf16[4,768,768]{2,1,0:T(8,128)(2,1)} %all-gather.5.cloned.1.call-done), kind=kOutput, calls=%fused_computation.7 | convolution fusion | flops 29000466432 | bytes 18874368 | tf_op jit(solution)/shard_map/qac,sqcd->asd/dot_general | solution.py:25
  215.5 12.1 %copy.15 = f32[768,4,768]{2,1,0:T(4,128)} copy(f32[768,4,768]{0,2,1:T(8,128)} %fusion.7) | data formatting | bytes 18874368 | tf_op jit(solution)/shard_map/qac,sqcd->asd/dot_general | solution.py:25
  227.6 0.0 copy-start.5
  227.6 0.0 copy-start.2
  227.6 0.0 copy-start.4
  227.6 0.0 copy-start.3
  227.6 0.0 copy-start.1
  227.6 0.0 all-reduce.3.cloned.1.call-update
  227.7 0.6 copy-done.5
  228.3 0.6 dynamic-slice
  229.5 0.0 copy-done.2
  229.5 0.1 dynamic_slice.10
  229.6 0.0 copy-done.4
  229.6 0.6 dynamic_slice.9
  230.2 0.6 iota_compare_fusion.1
  230.8 0.0 copy-done
  230.8 0.1 constant_dynamic-slice_fusion
  230.9 0.0 copy-done.3
  230.9 0.2 select_reduce_fusion
  231.1 0.1 broadcast_add_fusion
  231.2 162.3 %all-reduce.3.cloned.1.call-done = f32[768,4,768]{2,1,0:T(4,128)} async-done(((f32[768,4,768]{2,1,0:T(4,128)}), f32[768,4,768]{2,1,0:T(4,128)}) %all-reduce.3.cloned.1.call-update) | async-done | bytes 9437200
  393.5 0.0 copy-done.1
  393.5 1.6 fusion.21
  395.1 0.7 copy.16
Async XLA Ops:
  6.5 224.3 %copy-start = (s32[32,2]{0,1:T(2,128)S(1)}, s32[32,2]{0,1:T(2,128)}, u32[]{:S(2)}) copy-start(s32[32,2]{0,1:T(2,128)} %param.9) | copy-start | bytes 772
  6.5 104.5 %all-gather.3.cloned.1.call-start = ((), (), s32[]{:S(2)}) async-start(), calls=%async_computation | async-start | bytes 5308416 | tf_op jit(solution)/shard_map/all_gather | solution.py:14
  7.3 165.5 %all-gather.5.cloned.1.call-start = ((), (), s32[]{:S(2)}) async-start(), calls=%async_computation.1 | async-start | bytes 5013504 | tf_op jit(solution)/shard_map/all_gather | solution.py:20
  8.0 385.5 %all-reduce.3.cloned.1.call-start = ((), (), s32[]{:S(2)}) async-start(), calls=%async_computation.2 | async-start | bytes 18874368
  227.6 0.7 copy-start.5
  227.6 1.9 copy-start.2
  227.6 2.0 copy-start.4
  227.6 3.3 copy-start.3
  227.6 165.9 %copy-start.1 = (bf16[4,48,768]{2,1,0:T(8,128)(2,1)S(1)}, bf16[4,48,768]{2,1,0:T(8,128)(2,1)}, u32[]{:S(2)}) copy-start(bf16[4,48,768]{2,1,0:T(8,128)(2,1)} %param.6) | copy-start | bytes 884740
Sparse Core Ops, SparseCore 0:
  9.0 102.0 all-gather.2
  113.5 59.1 all-gather.4
  227.8 165.7 all-reduce.2
where the time goes:
time: 403 us; the launch traced here: 402 us
  waiting for transfers between devices  328 us (81%)
  matrix products  42.8 us (11%)
  local copies, waits for them, and re-layouts  14.7 us (4%)
  between operations  13.8 us (3%)
    unnamed x4, waiting for transfers between devices  164 us
    all_gather x1, waiting for transfers between devices, per_device(): full_factors = lax.all_gather(factors, 'row', axis=1, tiled=True)  103 us
    all_gather x1, waiting for transfers between devices, per_device(): lax.all_gather(amplitudes, 'col', axis=1, tiled=True)  61.7 us
    dot_general x1, matrix products, per_device(): jnp.einsum('qac,sqcd->asd', full_factors, halfway, preferred_element_type...  42.8 us
    dot_general x1, local copies, waits for them, and re-layouts, per_device(): jnp.einsum('qac,sqcd->asd', full_factors, halfway, preferred_element_type...  12.1 us
  transfers between devices with their start and end apart: 3, of which 3 were waited for; matrix products, arithmetic and copies ran while one was open for 1% of the time, Pallas kernels for 0%

commit v1 on v0

--- a/solution.py
+++ b/solution.py
@@ -11,7 +11,9 @@
     col_rows = amplitudes.shape[1]
     row_id = lax.axis_index("row")
     col_id = lax.axis_index("col")
-    full_factors = lax.all_gather(factors, "row", axis=1, tiled=True)
+    full_factors = jnp.concatenate(
+        lax.all_to_all(jnp.stack([factors] * lax.axis_size("row")), "row", 0, 0), axis=1
+    )
     local_slots = jnp.arange(slot_count, dtype=jnp.int32)
     own_live = local_slots < counts[row_id]
     held_pairs = lax.dynamic_slice_in_dim(pair_index, row_id * slot_count, slot_count, 0)

time: 403 us -> 326 us (0.81)
  waiting for transfers between devices: 328 us -> 182 us
  blocking collectives: 0 us -> 65.1 us
  local copies, waits for them, and re-layouts: 14.7 us -> 18.8 us
    all_gather x1 -> x0, waiting for transfers between devices: 103 us -> none  [per_device(): full_factors = lax.all_gather(factors, 'row', axis=1, tiled=True)]
    all_to_all x0 -> x1, blocking collectives: none -> 65.1 us  [per_device(): lax.all_to_all(jnp.stack([factors] * lax.axis_size('row')), 'row', 0, 0)]
    all_gather x1, waiting for transfers between devices: 61.7 us -> 18.6 us  [per_device(): lax.all_gather(amplitudes, 'col', axis=1, tiled=True)]
    unnamed x4 -> x3, waiting for transfers between devices: 164 us -> 163 us
  transfers between devices with their start and end apart: 3 -> 2, of which waited for: 3 -> 2; matrix products, arithmetic and copies ran while one was open for 1% -> 2% of each run, Pallas kernels for 0% -> 0%
where the time goes in v1:
time: 326 us; the launch traced here: 325 us
  waiting for transfers between devices  182 us (56%)
  blocking collectives  65.1 us (20%)
  matrix products  42.8 us (13%)
  local copies, waits for them, and re-layouts  18.8 us (6%)
  between operations  14.1 us (4%)
    unnamed x3, waiting for transfers between devices  163 us
    all_to_all x1, blocking collectives, per_device(): lax.all_to_all(jnp.stack([factors] * lax.axis_size('row')), 'row', 0, 0)  65.1 us
    dot_general x1, matrix products, per_device(): jnp.einsum('qac,sqcd->asd', full_factors, halfway, preferred_element_type...  42.8 us
    all_gather x1, waiting for transfers between devices, per_device(): lax.all_gather(amplitudes, 'col', axis=1, tiled=True)  18.6 us
    dot_general x1, local copies, waits for them, and re-layouts, per_device(): jnp.einsum('qac,sqcd->asd', full_factors, halfway, preferred_element_type...  12.1 us
  transfers between devices with their start and end apart: 2, of which 2 were waited for; matrix products, arithmetic and copies ran while one was open for 2% of the time, Pallas kernels for 0%

profile of v1, /device:TPU:0, one launch (start us, length us, event | category | flops | bytes accessed | tf_op | source)
XLA Modules:
  0.0 325.3 jit_solution(12509260164452891044)
XLA Ops:
  6.5 0.0 copy-start
  6.5 0.0 all-gather.2.cloned.1.call-start
  6.5 0.7 all-gather.2.cloned.1.call-update
  7.3 0.0 all-reduce.3.cloned.1.call-start
  7.3 1.6 stack.2
  8.9 65.1 %all_to_all.5 = bf16[8,4,96,768]{3,2,1,0:T(8,128)(2,1)S(1)} all-to-all(bf16[8,4,96,768]{3,2,1,0:T(8,128)(2,1)S(1)} %stack.2), channel_id=1, replica_groups=mesh['row'=8,'col'=16] {'row'}, dimensions={0} | all-to-all | bytes 9437184 | tf_op jit(solution)/shard_map/all_to_all | solution.py:15
  74.0 2.5 copy.16
  76.5 18.6 %all-gather.2.cloned.1.call-done = bf16[4,768,768]{2,1,0:T(8,128)(2,1)} async-done(((bf16[4,48,768]{2,1,0:T(8,128)(2,1)}), bf16[4,768,768]{2,1,0:T(8,128)(2,1)}) %all-gather.2.cloned.1.call-update) | async-done | bytes 4718608 | tf_op jit(solution)/shard_map/all_gather | solution.py:22
  95.2 42.8 %fusion.5 = f32[768,4,768]{0,2,1:T(8,128)} fusion(bf16[4,768,768,1]{2,1,0,3:T(8,128)(2,1)} %bitcast.32, bf16[4,768,768]{2,1,0:T(8,128)(2,1)} %all-gather.2.cloned.1.call-done), kind=kOutput, calls=%fused_computation.5 | convolution fusion | flops 29000466432 | bytes 18874368 | tf_op jit(solution)/shard_map/qac,sqcd->asd/dot_general | solution.py:27
  138.0 12.1 %copy.17 = f32[768,4,768]{2,1,0:T(4,128)} copy(f32[768,4,768]{0,2,1:T(8,128)} %fusion.5) | data formatting | bytes 18874368 | tf_op jit(solution)/shard_map/qac,sqcd->asd/dot_general | solution.py:27
  150.1 0.0 copy-start.5
  150.1 0.0 copy-start.2
  150.1 0.0 copy-start.4
  150.1 0.0 copy-start.3
  150.1 0.0 copy-start.1
  150.1 0.0 all-reduce.3.cloned.1.call-update
  150.1 0.6 copy-done.5
  150.7 0.6 dynamic-slice
  152.0 0.0 copy-done.2
  152.0 0.1 dynamic_slice.10
  152.0 0.0 copy-done.4
  152.0 0.6 dynamic_slice.9
  152.6 0.6 iota_compare_fusion.1
  153.3 0.0 copy-done
  153.3 0.1 constant_dynamic-slice_fusion
  153.4 0.0 copy-done.3
  153.4 0.2 select_reduce_fusion
  153.6 0.1 broadcast_add_fusion
  153.6 162.5 %all-reduce.3.cloned.1.call-done = f32[768,4,768]{2,1,0:T(4,128)} async-done(((f32[768,4,768]{2,1,0:T(4,128)}), f32[768,4,768]{2,1,0:T(4,128)}) %all-reduce.3.cloned.1.call-update) | async-done | bytes 9437200
  316.1 0.0 copy-done.1
  316.1 1.6 fusion.13
  317.7 0.7 copy.18
Async XLA Ops:
  6.5 146.8 %copy-start = (s32[32,2]{0,1:T(2,128)S(1)}, s32[32,2]{0,1:T(2,128)}, u32[]{:S(2)}) copy-start(s32[32,2]{0,1:T(2,128)} %param.9) | copy-start | bytes 772
  6.5 88.6 %all-gather.2.cloned.1.call-start = ((), (), s32[]{:S(2)}) async-start(), calls=%async_computation.1 | async-start | bytes 5013504 | tf_op jit(solution)/shard_map/all_gather | solution.py:22
  7.3 308.9 %all-reduce.3.cloned.1.call-start = ((), (), s32[]{:S(2)}) async-start(), calls=%async_computation.2 | async-start | bytes 18874368
  150.1 0.7 copy-start.5
  150.1 1.9 copy-start.2
  150.1 2.0 copy-start.4
  150.1 3.3 %copy-start.3 = (f32[24]{0:T(128)S(1)}, f32[24]{0:T(128)}, u32[]{:S(2)}) copy-start(f32[24]{0:T(128)} %param.10) | copy-start | bytes 292
  150.1 166.1 %copy-start.1 = (bf16[4,48,768]{2,1,0:T(8,128)(2,1)S(1)}, bf16[4,48,768]{2,1,0:T(8,128)(2,1)}, u32[]{:S(2)}) copy-start(bf16[4,48,768]{2,1,0:T(8,128)(2,1)} %param.6) | copy-start | bytes 884740
Sparse Core Ops, SparseCore 0:
  9.8 85.3 all-gather.1
  150.2 165.8 all-reduce.2
